TPU v7x, 32 devices: a whole 2x2x4 slice. The times are simulated.
32 devices in a mesh: dp: 32 (over z, y, x, core).
Axes of the slice: x: 2, y: 2, z: 4, core: 2. Of those that a mesh axis runs over, the one named last changes fastest.
Arguments:
- patches: bfloat16 [32768, 1664], P('dp')
- ln_gain: float32 [1664], replicated, may hold values from 0.25 to 1.75
- w_qkv: bfloat16 [1664, 2496], P('dp')
- w_out: bfloat16 [832, 1664], P(None, 'dp'), may hold values from -0.21875 to 0.21875
- w_proj: bfloat16 [6656, 2048], P('dp'), may hold values from -0.078125 to 0.078125
- seg_ids: int32 [32768], P('dp'), may hold values from 0 to 4, as said below
- patch_mask: int32 [32768], P('dp'), may hold values 0 or 1
- grid_hw: int32 [128, 2], P('dp'), may hold values from 12 to 16, as said below
- owners: int32 [128], P('dp'), may hold values from 0 to 31
Outputs:
- routed: bfloat16 [8192, 2048], P('dp')
- image_rms: float32 [128], P('dp')
- image_max_logit: float32 [128], P('dp')
Inputs may be any that keep to these rules, and one draw needn't show every extreme that they name: `seg_ids`: within each pack the images' tokens lie in order without gaps from the pack's first token, each image taking grid height times width consecutive tokens with segment numbers 0 to 3; the remaining tokens carry 4. `grid_hw`: heights and widths are 12, 14 or 16; every pack has an image of 16 x 16 patches, so an image has at most 64 merged rows, and every pack also has an image of height 12.
All inputs are finite; a program needn't handle non-finite values. No bound on the sum of `patch_mask` on one device may be relied on, other than what follows from the above.
Results may differ from a plain program's by a relative error of at most 0.006.
Values may be sent and summed in bfloat16 or wider, within the bound.
A program may use at most 192 MiB of HBM per device.

v0:
```python
import jax
import jax.numpy as jnp
from jax import lax
from jax.sharding import PartitionSpec as P

HEADS = 8
CAP = 64


def token_places(seg_row, grid_rows):
    heights = grid_rows[:, 0]
    widths = grid_rows[:, 1]
    areas = heights * widths
    ends_at = jnp.cumsum(areas)
    starts = ends_at - areas
    image_count = grid_rows.shape[0]
    member = seg_row[:, None] == jnp.arange(image_count, dtype=jnp.int32)[None, :]
    start_tok = jnp.sum(jnp.where(member, starts[None, :], 0), axis=1)
    half_w = jnp.maximum(jnp.sum(jnp.where(member, (widths // 2)[None, :], 0), axis=1), 1)
    offset = jnp.arange(seg_row.shape[0], dtype=jnp.int32) - start_tok
    window = offset // 4
    corner = offset % 4
    row_pos = 2 * (window // half_w) + corner // 2
    col_pos = 2 * (window % half_w) + corner % 2
    return (row_pos.astype(jnp.float32), col_pos.astype(jnp.float32), areas, starts)


def rotate(heads_in, row_pos, col_pos):
    quarter = heads_in.shape[-1] // 4
    theta = 100.0 ** (-jnp.arange(quarter, dtype=jnp.float32) / quarter)
    out_parts = []
    for which_pos, offset_at in ((row_pos, 0), (col_pos, 2 * quarter)):
        angles = (which_pos[:, None] * theta[None, :])[:, None, :]
        cosine = jnp.cos(angles)
        sine_val = jnp.sin(angles)
        part_a = heads_in[..., offset_at : offset_at + quarter]
        part_b = heads_in[..., offset_at + quarter : offset_at + 2 * quarter]
        out_parts += [part_a * cosine - part_b * sine_val, part_a * sine_val + part_b * cosine]
    return jnp.concatenate(out_parts, axis=-1)


def send_rows(proj_bf, starts, areas, owner_row, device_count):
    merged_rows = proj_bf.shape[0]
    wrap_count = (CAP + device_count - 1) // device_count
    dest_ids = jnp.arange(device_count, dtype=jnp.int32)[:, None, None]
    wrap_ids = jnp.arange(wrap_count, dtype=jnp.int32)[None, None, :]
    owner_here = owner_row[None, :, None]
    row_within = wrap_ids * device_count + (dest_ids - owner_here) % device_count
    row_total = (areas // 4)[None, :, None]
    first_row = (starts // 4)[None, :, None]
    picked = jnp.where(row_within < row_total, first_row + row_within, merged_rows)
    padded = jnp.concatenate([proj_bf, jnp.zeros((1, proj_bf.shape[1]), proj_bf.dtype)], axis=0)
    return padded[picked]


def attend(queries, key_rows, values, seg_query, seg_key, mask_key, query_at):
    scores = jnp.einsum(
        "qhd,khd->hqk", queries, key_rows, preferred_element_type=jnp.float32
    ) * queries.shape[-1] ** (-0.5)
    query_idx = query_at + jnp.arange(queries.shape[0], dtype=jnp.int32)
    key_idx = jnp.arange(key_rows.shape[0], dtype=jnp.int32)
    allowed = (seg_query[:, None] == seg_key[None, :]) & (
        (mask_key[None, :] == 1) | (query_idx[:, None] == key_idx[None, :])
    )
    masked = jnp.where(allowed[None], scores, -1e30)
    top_row = jnp.max(masked, axis=-1, keepdims=True)
    expo = jnp.where(allowed[None], jnp.exp(masked - top_row), 0.0)
    weights = (expo / jnp.sum(expo, axis=-1, keepdims=True)).astype(jnp.bfloat16)
    result = jnp.einsum("hqk,khd->qhd", weights, values, preferred_element_type=jnp.float32).astype(
        jnp.bfloat16
    )
    return (result.reshape(queries.shape[0], -1), jnp.max(top_row[..., 0], axis=0))


def on_device(patches, ln_gain, w_qkv, w_out, w_proj, seg_ids, patch_mask, grid_hw, owners):
    tok_count, width_in = patches.shape
    hidden_w = w_out.shape[0]
    image_count = grid_hw.shape[0]
    proj_w = w_proj.shape[1]
    tokens_f = patches.astype(jnp.float32)
    mean_row = jnp.mean(tokens_f, axis=-1, keepdims=True)
    centered = tokens_f - mean_row
    var_row = jnp.mean(centered * centered, axis=-1, keepdims=True)
    normed = (centered * lax.rsqrt(var_row + 1e-06) * ln_gain).astype(jnp.bfloat16)
    columns = normed
    mixed = jnp.dot(
        columns, lax.all_gather(w_qkv, "dp", axis=0, tiled=True), preferred_element_type=jnp.float32
    )
    row_pos, col_pos, areas, starts = token_places(seg_ids, grid_hw)
    shape_three = (tok_count, HEADS, hidden_w // HEADS)
    queries = rotate(mixed[:, :hidden_w].reshape(shape_three), row_pos, col_pos).astype(
        jnp.bfloat16
    )
    key_rows = rotate(
        mixed[:, hidden_w : 2 * hidden_w].reshape(shape_three), row_pos, col_pos
    ).astype(jnp.bfloat16)
    values = mixed[:, 2 * hidden_w :].reshape(shape_three).astype(jnp.bfloat16)
    image_ids = jnp.arange(image_count, dtype=jnp.int32)
    block_len = min(512, tok_count)
    outputs = []
    top_logit = jnp.full((image_count,), -1e30, jnp.float32)
    for block_idx in range(tok_count // block_len):
        query_at = block_idx * block_len
        seg_query = seg_ids[query_at : query_at + block_len]
        block_out, row_top = attend(
            queries[query_at : query_at + block_len],
            key_rows,
            values,
            seg_query,
            seg_ids,
            patch_mask,
            query_at,
        )
        outputs.append(block_out)
        member_q = seg_query[:, None] == image_ids[None, :]
        top_logit = jnp.maximum(
            top_logit, jnp.max(jnp.where(member_q, row_top[:, None], -1e30), axis=0)
        )
    attended = jnp.concatenate(outputs, axis=0)
    out_term = jnp.dot(
        attended,
        lax.all_gather(w_out, "dp", axis=1, tiled=True),
        preferred_element_type=jnp.float32,
    )
    residual = (tokens_f + out_term).astype(jnp.bfloat16)
    merged = residual.reshape(tok_count // 4, 4 * width_in)
    columns = merged
    projected = jnp.dot(
        columns,
        lax.all_gather(w_proj, "dp", axis=0, tiled=True),
        preferred_element_type=jnp.float32,
    )
    proj_bf = projected.astype(jnp.bfloat16)
    merged_seg = seg_ids.reshape(-1, 4)[:, 0]
    member_m = merged_seg[:, None] == image_ids[None, :]
    squares = jnp.sum(projected * projected, axis=1)
    totals = jnp.sum(jnp.where(member_m, squares[:, None], 0.0), axis=0)
    image_rms = jnp.sqrt(totals / (areas // 4 * proj_w).astype(jnp.float32))
    sent = send_rows(proj_bf, starts, areas, owners, lax.axis_size("dp"))
    arrived = lax.all_to_all(sent, "dp", split_axis=0, concat_axis=0, tiled=True)
    return (arrived.reshape(-1, proj_w), image_rms, top_logit)


def solution(mesh):
    return jax.shard_map(
        on_device,
        mesh=mesh,
        in_specs=(
            P("dp", None),
            P(),
            P("dp", None),
            P(None, "dp"),
            P("dp", None),
            P("dp"),
            P("dp"),
            P("dp", None),
            P("dp"),
        ),
        out_specs=(P("dp", None), P("dp"), P("dp")),
        check_vma=False,
    )
```

profile of v0, /device:TPU:0, one launch (start us, length us, event | category | flops | bytes accessed | tf_op | source)
XLA Modules:
  0.0 377.8 jit_solution(15820809484206166901)
XLA Ops:
  15.9 2.5 convert_reduce_fusion
  20.2 2.3 multiply_cosine_fusion.1
  22.5 2.2 fusion.26
  24.7 48.0 %all-gather.10.cloned.1.call-done = bf16[32,52,832]{2,1,0:T(8,128)(2,1)} async-done(((bf16[1,52,832]{2,1,0:T(8,128)(2,1)}), bf16[32,52,832]{2,1,0:T(8,128)(2,1)}) %all-gather.10.cloned.1.call-update) | async-done | bytes 2768912 | tf_op jit(solution)/shard_map/all_gather | solution.py:122
  72.8 5.6 %reshape.553 = bf16[1664,832]{1,0:T(8,128)(2,1)} reshape(bf16[32,52,832]{2,1,0:T(8,128)(2,1)} %all-gather.10.cloned.1.call-done) | data formatting | bytes 5537792
  78.4 76.9 %all-gather.8.cloned.1.call-done = bf16[32,52,2496]{2,1,0:T(8,128)(2,1)} async-done(((bf16[1,52,2496]{2,1,0:T(8,128)(2,1)}), bf16[32,52,2496]{2,1,0:T(8,128)(2,1)}) %all-gather.8.cloned.1.call-update) | async-done | bytes 8306704 | tf_op jit(solution)/shard_map/all_gather | solution.py:87
  155.2 13.5 %reshape.551 = bf16[1664,2496]{1,0:T(8,128)(2,1)} reshape(bf16[32,52,2496]{2,1,0:T(8,128)(2,1)} %all-gather.8.cloned.1.call-done) | data formatting | bytes 16613376
  168.8 13.4 %fusion.20 = f32[1024,2496]{0,1:T(8,128)S(1)} fusion(bf16[1664,2496]{1,0:T(8,128)(2,1)} %reshape.551, bf16[1024,1664]{1,0:T(8,128)(2,1)S(1)} %copy-done, f32[1664]{0:T(1024)} %param.10, f32[1024]{0:T(1024)} %add_rsqrt_fusion, f32[1024]{0:T(1024)} %copy-done.17), kind=kOutput, calls=%fused_computation.30 | convolution fusion | flops 8514568192 | bytes 21953024 | tf_op jit(solution)/shard_map/dot_general | solution.py:86
  182.2 1.5 slice.130
  185.9 1.8 pad_maximum_fusion
  187.7 2.2 subtract_convert_fusion.1
  190.0 13.5 %fusion.73 = (f32[8,512]{1,0:T(8,128)S(1)}, f32[8,512,1024]{2,1,0:T(8,128)}) fusion(pred[512,1024]{1,0:T(8,128)(4,1)} %get-tuple-element.27, bf16[1024,8,104]{0,2,1:T(8,128)(2,1)} %pad_maximum_fusion, bf16[1024,8,26]{0,2,1:T(8,128)(2,1)} %get-tuple-element.19, bf16[1024,8,26]{0,2,1:T(8,128)(2,1)} %get-tuple-element.20, ...), kind=kOutput, calls=%fused_computation.153 | convolution fusion | flops 900203520 | bytes 20791296 | tf_op jit(solution)/shard_map/sub | solution.py:67
  203.5 13.3 %fusion.70 = (f32[8,512]{1,0:T(8,128)S(1)}, f32[8,512,1024]{2,1,0:T(8,128)}) fusion(pred[512,1024]{1,0:T(8,128)(4,1)} %get-tuple-element.28, bf16[1024,8,104]{0,2,1:T(8,128)(2,1)} %pad_maximum_fusion, bf16[1024,8,26]{0,2,1:T(8,128)(2,1)} %get-tuple-element.19, bf16[1024,8,26]{0,2,1:T(8,128)(2,1)} %get-tuple-element.20, ...), kind=kOutput, calls=%fused_computation.152 | convolution fusion | flops 900203520 | bytes 20791296 | tf_op jit(solution)/shard_map/sub | solution.py:67
  216.8 8.1 %fusion.37 = bf16[8,104,512]{2,1,0:T(8,128)(2,1)S(1)} fusion(bf16[1024,8,104]{0,2,1:T(8,128)(2,1)} %bitcast.49, f32[8,512,1024]{2,1,0:T(8,128)} %get-tuple-element.41, f32[8,512]{1,0:T(8,128)S(1)} %get-tuple-element.40), kind=kOutput, calls=%fused_computation.50 | convolution fusion | flops 881229824 | bytes 19349504 | tf_op jit(solution)/shard_map/hqk,khd->qhd/dot_general | solution.py:69
  224.9 7.5 %fusion.36 = bf16[8,104,512]{2,1,0:T(8,128)(2,1)S(1)} fusion(bf16[1024,8,104]{0,2,1:T(8,128)(2,1)S(1)} %bitcast.50, f32[8,512,1024]{2,1,0:T(8,128)} %get-tuple-element.39, f32[8,512]{1,0:T(8,128)S(1)} %get-tuple-element.38), kind=kOutput, calls=%fused_computation.49 | convolution fusion | flops 881229824 | bytes 19349504 | tf_op jit(solution)/shard_map/hqk,khd->qhd/dot_general | solution.py:69
  232.5 6.0 %fusion.19 = bf16[1024,1664]{1,0:T(8,128)(2,1)} fusion(bf16[1024,1664]{1,0:T(8,128)(2,1)S(1)} %copy-done, bf16[1664,832]{1,0:T(8,128)(2,1)S(1)} %copy-done.1, bf16[512,832]{0,1:T(8,128)(2,1)S(1)} %bitcast.54, bf16[512,832]{0,1:T(8,128)(2,1)S(1)} %bitcast.53), kind=kOutput, calls=%fused_computation.29 | convolution fusion | flops 2843869184 | bytes 11288576 | tf_op jit(solution)/shard_map/dot_general | solution.py:120
  238.4 5.9 %reshape.538 = bf16[256,6656]{1,0:T(8,128)(2,1)S(1)} reshape(bf16[1024,1664]{1,0:T(8,128)(2,1)} %fusion.19) | data formatting | bytes 6815744 | tf_op jit(solution)/shard_map/reshape | solution.py:126
  244.4 77.0 %all-gather.6.cloned.1.call-done = bf16[6656,2048]{1,0:T(8,128)(2,1)} async-done(((bf16[208,2048]{1,0:T(8,128)(2,1)}), bf16[6656,2048]{1,0:T(8,128)(2,1)}) %all-gather.6.cloned.1.call-update) | async-done | bytes 27262992 | tf_op jit(solution)/shard_map/all_gather | solution.py:130
  321.4 14.0 %multiply_reduce_fusion = (f32[256]{0:T(256)S(1)}, bf16[256,2048]{1,0:T(8,128)(2,1)}) fusion(bf16[256,6656]{1,0:T(8,128)(2,1)S(1)} %reshape.538, bf16[6656,2048]{1,0:T(8,128)(2,1)} %all-gather.6.cloned.1.call-done), kind=kOutput, calls=%fused_computation.35 | convolution fusion | flops 6980894720 | bytes 31720448 | tf_op jit(solution)/shard_map/dot_general | solution.py:128
  339.0 1.5 reshape.542
  340.5 3.0 all-to-all-start
  343.6 5.6 %fusion.2 = f32[512]{0:T(512)S(1)} fusion(pred[512,1024]{1,0:T(8,128)(4,1)} %get-tuple-element.27, bf16[1024,8,26]{0,2,1:T(8,128)(2,1)} %get-tuple-element.19, bf16[1024,8,26]{0,2,1:T(8,128)(2,1)} %get-tuple-element.20, bf16[1024,8,26]{0,2,1:T(8,128)(2,1)} %get-tuple-element.12, bf16[1024,8,26]{0,2,1:T(8,128)(2,1)} %get-tuple-element.11, ...), kind=kOutput, calls=%fused_computation.9 | convolution fusion | flops 891813376 | bytes 3475456 | tf_op jit(solution)/shard_map/qhd,khd->hqk/dot_general | solution.py:57
  349.3 4.0 %fusion.4 = f32[512]{0:T(512)S(1)} fusion(pred[512,1024]{1,0:T(8,128)(4,1)S(1)} %copy-done.7, bf16[1024,8,26]{0,2,1:T(8,128)(2,1)S(1)} %copy-done.10, bf16[1024,8,26]{0,2,1:T(8,128)(2,1)S(1)} %copy-done.11, bf16[1024,8,26]{0,2,1:T(8,128)(2,1)S(1)} %copy-done.9, bf16[1024,8,26]{0,2,1:T(8,128)(2,1)S(1)} %copy-done.8, bf16[1024,8,104]{0,2,1:T(8,128)(2,1)S(1)} %copy-done.2), kind=kOutput, calls=%fused_computation.11 | convolution fusion | flops 891813376 | bytes 3475456 | tf_op jit(solution)/shard_map/qhd,khd->hqk/dot_general | solution.py:57
  354.0 15.8 %all-to-all-done = bf16[32,4,2,2048]{3,2,1,0:T(2,128)(2,1)S(1)} async-done(((bf16[32,4,2,2048]{3,2,1,0:T(2,128)(2,1)}), bf16[32,4,2,2048]{3,2,1,0:T(2,128)(2,1)S(1)}, u32[]{:S(2)}, u32[]{:S(2)}) %all-to-all-start) | async-done | bytes 1048608 | tf_op jit(solution)/shard_map/all_to_all | solution.py:140
  (80 shorter events, 18.2 us)
Async XLA Ops:
  7.2 11.3 %copy-start = (bf16[1024,1664]{1,0:T(8,128)(2,1)S(1)}, bf16[1024,1664]{1,0:T(8,128)(2,1)}, u32[]{:S(2)}) copy-start(bf16[1024,1664]{1,0:T(8,128)(2,1)} %param.9) | copy-start | bytes 10223620
  7.2 65.6 %all-gather.10.cloned.1.call-start = ((), (), s32[]{:S(2)}) async-start(), calls=%async_computation.3 | async-start | bytes 3311616 | tf_op jit(solution)/shard_map/all_gather | solution.py:122
  7.9 147.3 %all-gather.8.cloned.1.call-start = ((), (), s32[]{:S(2)}) async-start(), calls=%async_computation.2 | async-start | bytes 9461760 | tf_op jit(solution)/shard_map/all_gather | solution.py:87
  8.7 312.7 %all-gather.6.cloned.1.call-start = ((), (), s32[]{:S(2)}) async-start(), calls=%async_computation.1 | async-start | bytes 28114944 | tf_op jit(solution)/shard_map/all_gather | solution.py:130
  15.9 6.6 %copy-start.13 = (s32[512]{0:T(512)}, s32[512]{0:T(512)S(1)}, u32[]{:S(2)}) copy-start(s32[512]{0:T(512)S(1)} %get-tuple-element.33) | copy-start | bytes 6148
  15.9 6.6 %copy-start.15 = (s32[512]{0:T(512)}, s32[512]{0:T(512)S(1)}, u32[]{:S(2)}) copy-start(s32[512]{0:T(512)S(1)} %get-tuple-element.34) | copy-start | bytes 6148
  15.9 4.3 %copy-start.22 = (s32[4]{0:T(128)S(1)}, s32[4]{0:T(128)}, u32[]{:S(2)}) copy-start(s32[4]{0:T(128)} %param.17) | copy-start | bytes 52
  15.9 6.6 %copy-start.12 = (s32[1024]{0:T(1024)S(1)}, s32[1024]{0:T(1024)}, u32[]{:S(2)}) copy-start(s32[1024]{0:T(1024)} %param.14) | copy-start | bytes 12292
  18.4 1.8 copy-start.17
  216.8 8.1 %copy-start.3 = (bf16[1024,832]{0,1:T(8,128)(2,1)S(1)}, bf16[1024,832]{0,1:T(8,128)(2,1)}, u32[]{:S(2)}) copy-start(bf16[1024,832]{0,1:T(8,128)(2,1)} %slice.130) | copy-start | bytes 5111812
  224.9 7.5 %copy-start.1 = (bf16[1664,832]{1,0:T(8,128)(2,1)S(1)}, bf16[1664,832]{1,0:T(8,128)(2,1)}, u32[]{:S(2)}) copy-start(bf16[1664,832]{1,0:T(8,128)(2,1)} %reshape.553) | copy-start | bytes 8306692
  244.3 91.0 %copy-start.18 = (s32[256]{0:T(256)S(1)}, s32[256]{0:T(256)}, u32[]{:S(2)}) copy-start(s32[256]{0:T(256)} %slice_reduce_fusion) | copy-start | bytes 3076
  244.3 91.1 %copy-start.19 = (s32[4,2]{0,1:T(2,128)S(1)}, s32[4,2]{0,1:T(2,128)}, u32[]{:S(2)}) copy-start(s32[4,2]{0,1:T(2,128)} %param.16) | copy-start | bytes 100
  244.3 91.7 %copy-start.20 = (s32[4]{0:T(128)S(1)}, s32[4]{0:T(128)}, u32[]{:S(2)}) copy-start(s32[4]{0:T(128)} %get-tuple-element.7) | copy-start | bytes 52
  244.4 91.6 %copy-start.21 = (s32[2]{0:T(128)S(1)}, s32[2]{0:T(128)}, u32[]{:S(2)}) copy-start(s32[2]{0:T(128)} %iota_multiply_fusion) | copy-start | bytes 28
  340.5 29.2 %all-to-all-start = ((bf16[32,4,2,2048]{3,2,1,0:T(2,128)(2,1)}), bf16[32,4,2,2048]{3,2,1,0:T(2,128)(2,1)S(1)}, u32[]{:S(2)}, u32[]{:S(2)}) async-start(bf16[32,4,2,2048]{3,2,1,0:T(2,128)(2,1)} %reshape.542), calls=%async_computation | async-start | bytes 2097152 | tf_op jit(solution)/shard_map/all_to_all | solution.py:140
  343.5 5.7 %copy-start.2 = (bf16[1024,8,104]{0,2,1:T(8,128)(2,1)S(1)}, bf16[1024,8,104]{0,2,1:T(8,128)(2,1)}, u32[]{:S(2)}) copy-start(bf16[1024,8,104]{0,2,1:T(8,128)(2,1)} %pad_maximum_fusion) | copy-start | bytes 5111812
  343.6 5.7 %copy-start.7 = (pred[512,1024]{1,0:T(8,128)(4,1)S(1)}, pred[512,1024]{1,0:T(8,128)(4,1)}, u32[]{:S(2)}) copy-start(pred[512,1024]{1,0:T(8,128)(4,1)} %get-tuple-element.28) | copy-start | bytes 1572868
  343.6 5.7 %copy-start.8 = (bf16[1024,8,26]{0,2,1:T(8,128)(2,1)S(1)}, bf16[1024,8,26]{0,2,1:T(8,128)(2,1)}, u32[]{:S(2)}) copy-start(bf16[1024,8,26]{0,2,1:T(8,128)(2,1)} %get-tuple-element.11) | copy-start | bytes 1277956
  343.6 5.7 %copy-start.9 = (bf16[1024,8,26]{0,2,1:T(8,128)(2,1)S(1)}, bf16[1024,8,26]{0,2,1:T(8,128)(2,1)}, u32[]{:S(2)}) copy-start(bf16[1024,8,26]{0,2,1:T(8,128)(2,1)} %get-tuple-element.12) | copy-start | bytes 1277956
  343.6 5.7 %copy-start.10 = (bf16[1024,8,26]{0,2,1:T(8,128)(2,1)S(1)}, bf16[1024,8,26]{0,2,1:T(8,128)(2,1)}, u32[]{:S(2)}) copy-start(bf16[1024,8,26]{0,2,1:T(8,128)(2,1)} %get-tuple-element.19) | copy-start | bytes 1277956
  343.6 5.7 %copy-start.11 = (bf16[1024,8,26]{0,2,1:T(8,128)(2,1)S(1)}, bf16[1024,8,26]{0,2,1:T(8,128)(2,1)}, u32[]{:S(2)}) copy-start(bf16[1024,8,26]{0,2,1:T(8,128)(2,1)} %get-tuple-element.20) | copy-start | bytes 1277956
  349.3 4.0 %copy-start.14 = (s32[512]{0:T(512)S(1)}, s32[512]{0:T(512)}, u32[]{:S(2)}) copy-start(s32[512]{0:T(512)} %copy-done.13) | copy-start | bytes 6148
  349.3 4.0 %copy-start.16 = (s32[512]{0:T(512)S(1)}, s32[512]{0:T(512)}, u32[]{:S(2)}) copy-start(s32[512]{0:T(512)} %copy-done.15) | copy-start | bytes 6148
  (3 other events, 3.8 us)
Sparse Core Ops, SparseCore 0:
  10.9 61.7 all-gather.9
  75.6 79.5 all-gather.7
  158.1 163.2 all-gather.5
where the time goes:
time: 381 us; the launch traced here: 378 us
  waiting for transfers between devices  220 us (58%)
  matrix products  85.4 us (22%)
  local copies, waits for them, and re-layouts  35.6 us (9%)
  other arithmetic  19.4 us (5%)
  between operations  14.4 us (4%)
    all_gather x1, waiting for transfers between devices, on_device(): lax.all_gather(w_proj, 'dp', axis=0, tiled=True)  77 us
    all_gather x1, waiting for transfers between devices, on_device(): lax.all_gather(w_qkv, 'dp', axis=0, tiled=True)  76.9 us
    all_gather x1, waiting for transfers between devices, on_device(): lax.all_gather(w_out, 'dp', axis=1, tiled=True)  48 us
    sub x2, matrix products, attend(): expo = jnp.where(allowed[None], jnp.exp(masked - top_row), 0.0)  26.8 us
    unnamed x48, local copies, waits for them, and re-layouts  19.3 us
    all_to_all x1, waiting for transfers between devices, on_device(): lax.all_to_all(sent, 'dp', split_axis=0, concat_axis=0, tiled=True)  15.8 us
    dot_general x2, matrix products, attend(): jnp.einsum('hqk,khd->qhd', weights, values, preferred_element_type=jnp.fl...  15.7 us
    dot_general x1, matrix products, on_device(): jnp.dot(columns, lax.all_gather(w_proj, 'dp', axis=0, tiled=True), prefer...  14 us
  transfers between devices with their start and end apart: 4, of which 4 were waited for; matrix products, arithmetic and copies ran while one was open for 32% of the time, Pallas kernels for 0%

commit v1 on v0

v1 whole, which is shorter than its diff:
```python
import functools

import jax
import jax.numpy as jnp
from jax import lax
from jax.experimental import pallas as pl
from jax.experimental.pallas import tpu as pltpu
from jax.sharding import PartitionSpec as P

HEADS = 8
CAP = 64
LANES = 128
MESH = pl.DeviceIdType.MESH


def token_places(seg_row, grid_rows):
    heights = grid_rows[:, 0]
    widths = grid_rows[:, 1]
    areas = heights * widths
    ends_at = jnp.cumsum(areas)
    starts = ends_at - areas
    image_count = grid_rows.shape[0]
    member = seg_row[:, None] == jnp.arange(image_count, dtype=jnp.int32)[None, :]
    start_tok = jnp.sum(jnp.where(member, starts[None, :], 0), axis=1)
    half_w = jnp.maximum(jnp.sum(jnp.where(member, (widths // 2)[None, :], 0), axis=1), 1)
    offset = jnp.arange(seg_row.shape[0], dtype=jnp.int32) - start_tok
    window = offset // 4
    corner = offset % 4
    row_pos = 2 * (window // half_w) + corner // 2
    col_pos = 2 * (window % half_w) + corner % 2
    return (row_pos.astype(jnp.float32), col_pos.astype(jnp.float32), areas, starts)


def rope_tables(row_pos, col_pos, head_dim):
    quarter = head_dim // 4
    lane = jnp.arange(LANES, dtype=jnp.int32)
    theta = 100.0 ** (-(lane % quarter).astype(jnp.float32) / quarter)
    part = lane // quarter
    pos = jnp.where(part[None, :] < 2, row_pos[:, None], col_pos[:, None])
    angles = pos * theta[None, :]
    cosine = jnp.cos(angles)
    sine = jnp.sin(angles)
    first = (part == 0) | (part == 2)
    second = (part == 1) | (part == 3)
    return (
        cosine,
        jnp.where(first[None, :], -sine, 0.0),
        jnp.where(second[None, :], sine, 0.0),
    )


def send_rows(proj_bf, starts, areas, owner_row, device_count):
    merged_rows = proj_bf.shape[0]
    wrap_count = (CAP + device_count - 1) // device_count
    dest_ids = jnp.arange(device_count, dtype=jnp.int32)[:, None, None]
    wrap_ids = jnp.arange(wrap_count, dtype=jnp.int32)[None, None, :]
    owner_here = owner_row[None, :, None]
    row_within = wrap_ids * device_count + (dest_ids - owner_here) % device_count
    row_total = (areas // 4)[None, :, None]
    first_row = (starts // 4)[None, :, None]
    picked = jnp.where(row_within < row_total, first_row + row_within, merged_rows)
    padded = jnp.concatenate([proj_bf, jnp.zeros((1, proj_bf.shape[1]), proj_bf.dtype)], axis=0)
    return padded[picked]


class Place:
    def __init__(self):
        me = lax.axis_index("dp")
        self.core = me % 2
        self.x = (me // 2) % 2
        self.y = (me // 4) % 2
        self.z = me // 8

    def line(self, r):
        z = self.z
        return (z, z + 1 - 2 * (z % 2), z + 2 - 4 * (z // 2), 3 - z)[r]

    def column(self, r, s):
        odd = (self.z + r) % 2
        x, y = self.x, self.y
        if s == 0:
            return y, x
        if s == 1:
            return y + odd * (1 - 2 * y), x + (1 - odd) * (1 - 2 * x)
        if s == 2:
            return y + (1 - odd) * (1 - 2 * y), x + odd * (1 - 2 * x)
        return 1 - y, 1 - x

    def chip(self, r, s):
        y, x = self.column(r, s)
        return (self.line(r) * 2 + y) * 2 + x

    def line_peer(self, r):
        return ((self.line(r) * 2 + self.y) * 2 + self.x) * 2 + self.core

    def side_peer(self, r, s):
        y, x = self.column(r, s)
        return ((self.z * 2 + y) * 2 + x) * 2 + self.core

    def twin(self):
        return ((self.z * 2 + self.y) * 2 + self.x) * 2 + 1 - self.core

    def greet(self):
        barrier = pltpu.get_barrier_semaphore()
        peers = [self.line_peer(r) for r in (1, 2, 3)]
        peers += [self.side_peer(0, 1), self.side_peer(0, 2), self.twin()]
        for peer in peers:
            pl.semaphore_signal(barrier, inc=1, device_id=(peer,), device_id_type=MESH)
        pl.semaphore_wait(barrier, len(peers))


class Gather:
    def __init__(self, place, src, dst_of, sems, at):
        self.place, self.src, self.dst_of = place, src, dst_of
        self.send, self.recv, self.twin_send, self.twin_recv, self.local = sems
        self.at = at
        self.ici = {}
        self.started = []

    def dst(self, r, s):
        return self.dst_of(self.place.chip(r, s))

    def remote(self, src, dst, send_sem, recv_sem, peer):
        copy = pltpu.make_async_remote_copy(
            src_ref=src,
            dst_ref=dst,
            send_sem=send_sem,
            recv_sem=recv_sem,
            device_id=(peer,),
            device_id_type=MESH,
        )
        copy.start()
        self.started.append(copy)
        return copy

    def over_links(self, src, unit, arrives, peer):
        n = self.at * 16 + arrives[0] * 4 + arrives[1]
        self.ici[arrives] = self.remote(
            src, self.dst(*unit), self.send.at[n], self.recv.at[n], peer
        )

    def to_twin(self, src, r, s):
        n = self.at * 16 + r * 4 + s
        self.twins.append(
            self.remote(
                src,
                self.dst(r, s),
                self.twin_send.at[n],
                self.twin_recv.at[n],
                self.place.twin(),
            )
        )

    def start(self):
        self.twins = []
        for r in (1, 2, 3):
            self.over_links(self.src, (0, 0), (r, 0), self.place.line_peer(r))
        self.spread(0)
        self.own = pltpu.make_async_copy(self.src, self.dst(0, 0), self.local.at[self.at])
        self.own.start()

    def spread(self, r):
        src = self.src if r == 0 else self.dst(r, 0)
        self.over_links(src, (r, 0), (r, 1), self.place.side_peer(r, 1))
        self.over_links(src, (r, 0), (r, 2), self.place.side_peer(r, 2))
        self.to_twin(src, r, 0)

    def second(self):
        for r in (1, 2, 3):
            self.ici[(r, 0)].wait_recv()
            self.spread(r)

    def third(self):
        for r in range(4):
            self.ici[(r, 1)].wait_recv()
            src = self.dst(r, 1)
            self.over_links(src, (r, 1), (r, 3), self.place.side_peer(r, 2))
            self.to_twin(src, r, 1)

    def fourth(self):
        for s in (2, 3):
            for r in range(4):
                self.ici[(r, s)].wait_recv()
                self.to_twin(self.dst(r, s), r, s)

    def finish(self):
        for copy in self.twins:
            copy.wait_recv()
        for copy in self.started:
            copy.wait_send()
        self.own.wait()


def gather_sems(chunks):
    return [pltpu.SemaphoreType.DMA((chunks * 16,))] * 4 + [pltpu.SemaphoreType.DMA((chunks,))]


def run_gathers(gathers, work):
    count = len(gathers)
    for step in range(count + 4):
        if step < count:
            gathers[step].start()
        work(step)
        if 0 <= step - 1 < count:
            gathers[step - 1].second()
        if 0 <= step - 2 < count:
            gathers[step - 2].third()
        if 0 <= step - 3 < count:
            gathers[step - 3].fourth()
        if 0 <= step - 4 < count:
            gathers[step - 4].finish()


def qkv_kernel(chunks, src_ref, out_ref, *sems):
    place = Place()
    place.greet()
    wide = src_ref.shape[1] // chunks
    gathers = []
    for q in range(chunks):
        cols = slice(q * wide, (q + 1) * wide)

        def dst_of(chip, cols=cols):
            return out_ref.at[place.core, chip, :, cols]

        gathers.append(Gather(place, src_ref.at[:, cols], dst_of, sems, q))
    run_gathers(gathers, lambda step: None)


def gather_qkv(block):
    rows, cols = block.shape
    chunks = 4
    return pl.pallas_call(
        functools.partial(qkv_kernel, chunks),
        out_shape=jax.ShapeDtypeStruct((2, 16, rows, cols), block.dtype),
        in_specs=[pl.BlockSpec(memory_space=pl.ANY)],
        out_specs=pl.BlockSpec(memory_space=pl.ANY),
        scratch_shapes=gather_sems(chunks),
        compiler_params=pltpu.CompilerParams(collective_id=0, has_side_effects=True),
    )(block)


def attend_kernel(
    chunks,
    scale,
    mixed_ref,
    cos_ref,
    sin_a_ref,
    sin_b_ref,
    seg_col_ref,
    seg_row_ref,
    mask_row_ref,
    wo_ref,
    wp_ref,
    att_ref,
    top_ref,
    wo_all,
    wp_all,
    q_buf,
    k_buf,
    v_buf,
    *sems,
):
    place = Place()
    place.greet()
    wide = wp_ref.shape[1] // chunks
    gathers = [
        Gather(place, wo_ref, lambda chip: wo_all.at[place.core, chip], sems, 0)
    ]
    for q in range(chunks):
        cols = slice(q * wide, (q + 1) * wide)

        def dst_of(chip, cols=cols):
            return wp_all.at[chip, place.core, :, cols]

        gathers.append(Gather(place, wp_ref.at[:, cols], dst_of, sems, q + 1))
    tokens = seg_col_ref.shape[0]
    block = 256
    half = HEADS // 2

    def turn(i, carry):
        rows = pl.ds(pl.multiple_of(i * block, block), block)
        cosine, sin_a, sin_b = cos_ref[rows, :], sin_a_ref[rows, :], sin_b_ref[rows, :]
        quarter = 26
        for h in range(HEADS):
            at = (h % half) * LANES
            out = slice(h * LANES, (h + 1) * LANES)
            for kind, buf in ((0, q_buf), (1, k_buf)):
                lanes = slice(kind * half * LANES + at, kind * half * LANES + at + LANES)
                val = mixed_ref[h // half, rows, lanes]
                turned = (
                    val * cosine
                    + pltpu.roll(val, LANES - quarter, 1) * sin_a
                    + pltpu.roll(val, quarter, 1) * sin_b
                )
                buf[rows, out] = turned.astype(jnp.bfloat16)
            lanes = slice(2 * half * LANES + at, 2 * half * LANES + at + LANES)
            v_buf[rows, out] = mixed_ref[h // half, rows, lanes].astype(jnp.bfloat16)
        return carry

    def one_block(i, carry):
        rows = pl.ds(pl.multiple_of(i * block, block), block)
        seg_q = seg_col_ref[rows, :]
        query_idx = i * block + lax.broadcasted_iota(jnp.int32, (block, tokens), 0)
        key_idx = lax.broadcasted_iota(jnp.int32, (block, tokens), 1)
        allowed = (seg_q == seg_row_ref[...]) & (
            (mask_row_ref[...] == 1) | (query_idx == key_idx)
        )
        bias = jnp.where(allowed, 0.0, -1e30)
        best = jnp.full((block, 1), -1e30, jnp.float32)
        for h in range(HEADS):
            lanes = slice(h * LANES, (h + 1) * LANES)
            scores = lax.dot_general(
                q_buf[rows, lanes],
                k_buf[:, lanes],
                (((1,), (1,)), ((), ())),
                preferred_element_type=jnp.float32,
            )
            scores = scores * scale + bias
            top = jnp.max(scores, axis=1, keepdims=True)
            best = jnp.maximum(best, top)
            expo = jnp.exp(scores - top)
            total = jnp.sum(expo, axis=1, keepdims=True)
            got = jnp.dot(
                expo.astype(jnp.bfloat16), v_buf[:, lanes], preferred_element_type=jnp.float32
            )
            att_ref[rows, lanes] = (got / total).astype(jnp.bfloat16)
        top_ref[rows, :] = jnp.broadcast_to(best, (block, LANES))
        return carry

    blocks = tokens // block

    def work(step):
        if step == 0:
            lax.fori_loop(0, blocks, turn, 0)
        elif step == 1:
            lax.fori_loop(0, blocks // 2, one_block, 0)
        elif step == 2:
            lax.fori_loop(blocks // 2, blocks, one_block, 0)

    run_gathers(gathers, work)


def attend_and_gather(mixed, tables, seg, mask, wo_block, w_proj, head_dim):
    tokens = seg.shape[0]
    chunks = 4
    wide = HEADS * LANES
    vmem = pl.BlockSpec(memory_space=pltpu.VMEM)
    hbm = pl.BlockSpec(memory_space=pl.ANY)
    return pl.pallas_call(
        functools.partial(attend_kernel, chunks, head_dim ** (-0.5)),
        out_shape=(
            jax.ShapeDtypeStruct((tokens, wide), jnp.bfloat16),
            jax.ShapeDtypeStruct((tokens, LANES), jnp.float32),
            jax.ShapeDtypeStruct((2, 16) + wo_block.shape, jnp.bfloat16),
            jax.ShapeDtypeStruct((16, 2) + w_proj.shape, jnp.bfloat16),
        ),
        in_specs=[vmem] * 7 + [hbm] * 2,
        out_specs=(vmem, vmem, hbm, hbm),
        scratch_shapes=[pltpu.VMEM((tokens, wide), jnp.bfloat16)] * 3 + gather_sems(chunks + 1),
        compiler_params=pltpu.CompilerParams(
            collective_id=1, has_side_effects=True, vmem_limit_bytes=48 * 1024 * 1024
        ),
    )(mixed, *tables, seg[:, None], seg[None, :], mask[None, :], wo_block, w_proj)


def pair_blocks(w_qkv, w_out, head_dim):
    core = lax.axis_index("dp") % 2
    rows = w_qkv.shape[0]
    half = HEADS // 2
    pad = LANES - head_dim
    mine = jnp.concatenate([w_qkv, w_out.T], axis=1)
    twin = [(i, i + 1 - 2 * (i % 2)) for i in range(lax.axis_size("dp"))]
    parts = mine.reshape(rows, 4, 2, half, head_dim)
    keep = jnp.where(core == 0, parts[:, :, 0], parts[:, :, 1])
    give = jnp.where(core == 0, parts[:, :, 1], parts[:, :, 0])
    got = lax.ppermute(give.reshape(rows, -1), "dp", twin).reshape(keep.shape)
    both = jnp.concatenate(
        [jnp.where(core == 0, keep, got), jnp.where(core == 0, got, keep)], axis=0
    )
    both = jnp.pad(both, ((0, 0), (0, 0), (0, 0), (0, pad))).reshape(2 * rows, 4, half * LANES)
    return both[:, :3].reshape(2 * rows, 3 * half * LANES), both[:, 3]


def plain_gathers(normed, tables, seg_ids, patch_mask, w_qkv, w_out, w_proj):
    tok_count = normed.shape[0]
    hidden_w = w_out.shape[0]
    head_dim = hidden_w // HEADS
    quarter = head_dim // 4
    mixed = jnp.dot(
        normed, lax.all_gather(w_qkv, "dp", axis=0, tiled=True), preferred_element_type=jnp.float32
    )
    shape_three = (tok_count, HEADS, head_dim)
    cosine, sin_a, sin_b = [t[:, None, :head_dim] for t in tables]

    def rotate(val):
        return (
            val * cosine
            + jnp.roll(val, -quarter, axis=2) * sin_a
            + jnp.roll(val, quarter, axis=2) * sin_b
        ).astype(jnp.bfloat16)

    queries = rotate(mixed[:, :hidden_w].reshape(shape_three))
    key_rows = rotate(mixed[:, hidden_w : 2 * hidden_w].reshape(shape_three))
    values = mixed[:, 2 * hidden_w :].reshape(shape_three).astype(jnp.bfloat16)
    scores = jnp.einsum("qhd,khd->hqk", queries, key_rows, preferred_element_type=jnp.float32)
    idx = jnp.arange(tok_count, dtype=jnp.int32)
    allowed = (seg_ids[:, None] == seg_ids[None, :]) & (
        (patch_mask[None, :] == 1) | (idx[:, None] == idx[None, :])
    )
    masked = jnp.where(allowed[None], scores * head_dim ** (-0.5), -1e30)
    weights = jax.nn.softmax(masked, axis=-1).astype(jnp.bfloat16)
    attended = jnp.einsum("hqk,khd->qhd", weights, values, preferred_element_type=jnp.float32)
    attended = attended.astype(jnp.bfloat16).reshape(tok_count, hidden_w)
    out_term = jnp.dot(
        attended,
        lax.all_gather(w_out, "dp", axis=1, tiled=True),
        preferred_element_type=jnp.float32,
    )
    return out_term, jnp.max(masked, axis=(0, 2)), lax.all_gather(w_proj, "dp", axis=0, tiled=True)


def chip_gathers(normed, tables, seg_ids, patch_mask, w_qkv, w_out, w_proj):
    head_dim = w_out.shape[0] // HEADS
    qkv_block, wo_block = pair_blocks(w_qkv, w_out, head_dim)
    wq = gather_qkv(qkv_block).reshape(2, -1, qkv_block.shape[1])
    mixed = jnp.stack(
        [jnp.dot(normed, wq[i], preferred_element_type=jnp.float32) for i in range(2)]
    )
    att, top, wo, wp = attend_and_gather(
        mixed, tables, seg_ids, patch_mask, wo_block, w_proj, head_dim
    )
    wo = wo.reshape(2, -1, wo_block.shape[1])
    span = wo.shape[2]
    dims = (((1,), (1,)), ((), ()))
    out_term = lax.dot_general(
        att[:, :span], wo[0], dims, preferred_element_type=jnp.float32
    ) + lax.dot_general(att[:, span:], wo[1], dims, preferred_element_type=jnp.float32)
    return out_term, top[:, 0], wp.reshape(-1, w_proj.shape[1])


def on_device(patches, ln_gain, w_qkv, w_out, w_proj, seg_ids, patch_mask, grid_hw, owners):
    tok_count, width_in = patches.shape
    head_dim = w_out.shape[0] // HEADS
    image_count = grid_hw.shape[0]
    proj_w = w_proj.shape[1]
    devices = lax.axis_size("dp")
    tokens_f = patches.astype(jnp.float32)
    mean_row = jnp.mean(tokens_f, axis=-1, keepdims=True)
    centered = tokens_f - mean_row
    var_row = jnp.mean(centered * centered, axis=-1, keepdims=True)
    normed = (centered * lax.rsqrt(var_row + 1e-06) * ln_gain).astype(jnp.bfloat16)
    row_pos, col_pos, areas, starts = token_places(seg_ids, grid_hw)
    tables = rope_tables(row_pos, col_pos, head_dim)
    image_ids = jnp.arange(image_count, dtype=jnp.int32)
    path = chip_gathers if devices == 32 else plain_gathers
    out_term, row_top, wp = path(normed, tables, seg_ids, patch_mask, w_qkv, w_out, w_proj)
    member_q = seg_ids[:, None] == image_ids[None, :]
    top_logit = jnp.max(jnp.where(member_q, row_top[:, None], -1e30), axis=0)
    residual = (tokens_f + out_term).astype(jnp.bfloat16)
    merged = residual.reshape(tok_count // 4, 4 * width_in)
    projected = jnp.dot(merged, wp, preferred_element_type=jnp.float32)
    proj_bf = projected.astype(jnp.bfloat16)
    merged_seg = seg_ids.reshape(-1, 4)[:, 0]
    member_m = merged_seg[:, None] == image_ids[None, :]
    squares = jnp.sum(projected * projected, axis=1)
    totals = jnp.sum(jnp.where(member_m, squares[:, None], 0.0), axis=0)
    image_rms = jnp.sqrt(totals / (areas // 4 * proj_w).astype(jnp.float32))
    sent = send_rows(proj_bf, starts, areas, owners, devices)
    arrived = lax.all_to_all(sent, "dp", split_axis=0, concat_axis=0, tiled=True)
    return (arrived.reshape(-1, proj_w), image_rms, top_logit)


def solution(mesh):
    return jax.shard_map(
        on_device,
        mesh=mesh,
        in_specs=(
            P("dp", None),
            P(),
            P("dp", None),
            P(None, "dp"),
            P("dp", None),
            P("dp"),
            P("dp"),
            P("dp", None),
            P("dp"),
        ),
        out_specs=(P("dp", None), P("dp"), P("dp")),
        check_vma=False,
    )
```

time: 381 us -> 332 us (0.87)
  Pallas kernels: 0 us -> 202 us
  waiting for transfers between devices: 220 us -> 25.4 us
  matrix products: 85.4 us -> 39.7 us
  between operations: 14.4 us -> 0.96 us
  other arithmetic: 19.4 us -> 23.3 us
    all_gather x3 -> x0, waiting for transfers between devices: 202 us -> none  [the longest x1 77 us: on_device(): lax.all_gather(w_proj, 'dp', axis=0, tiled=True)]
    pallas_call x0 -> x2, Pallas kernels: none -> 202 us  [the longest x1 148 us: attend_and_gather(): pl.pallas_call(functools.partial(attend_kernel, chunks, head_dim ** (-0.5...]
    sub x2 -> x0, matrix products: 26.8 us -> none  [attend(): expo = jnp.where(allowed[None], jnp.exp(masked - top_row), 0.0)]
    unnamed x48 -> x21, local copies, waits for them, and re-layouts: 19.3 us -> 0.07 us
    dot_general x7 -> x5, matrix products: 58.6 us -> 39.7 us  [the longest x2 19.5 us: chip_gathers(): jnp.dot(normed, wq[i], preferred_element_type=jnp.float32)]
    all_to_all x1, waiting for transfers between devices: 15.8 us -> 25.4 us  [on_device(): lax.all_to_all(sent, 'dp', split_axis=0, concat_axis=0, tiled=True)]
    slice x3 -> x5, local copies, waits for them, and re-layouts: 3.48 us -> 11.5 us  [the longest x1 8.54 us: chip_gathers(): wq[i]]
    another operation x3 -> x2, other arithmetic: 3.34 us -> 10.6 us  [the longest x1 10.4 us: chip_gathers(): jnp.stack([jnp.dot(normed, wq[i], preferred_element_type=jnp.float32) for...]
  transfers between devices with their start and end apart: 4 -> 2, of which waited for: 4 -> 1; matrix products, arithmetic and copies ran while one was open for 32% -> 2% of each run, Pallas kernels for 0% -> 0%
where the time goes in v1:
time: 332 us; the launch traced here: 331 us
  Pallas kernels  202 us (61%)
  matrix products  39.7 us (12%)
  local copies, waits for them, and re-layouts  33.3 us (10%)
  waiting for transfers between devices  25.4 us (8%)
  other arithmetic  23.3 us (7%)
  starting transfers between devices  6.82 us (2%)
    pallas_call x1, Pallas kernels, attend_and_gather(): pl.pallas_call(functools.partial(attend_kernel, chunks, head_dim ** (-0.5...  148 us
    pallas_call x1, Pallas kernels, gather_qkv(): pl.pallas_call(functools.partial(qkv_kernel, chunks), out_shape=jax.Shape...  54 us
    all_to_all x1, waiting for transfers between devices, on_device(): lax.all_to_all(sent, 'dp', split_axis=0, concat_axis=0, tiled=True)  25.4 us
    dot_general x2, matrix products, chip_gathers(): jnp.dot(normed, wq[i], preferred_element_type=jnp.float32)  19.5 us
    dot_general x1, matrix products, on_device(): projected = jnp.dot(merged, wp, preferred_element_type=jnp.float32)  14.2 us
    another operation x1, other arithmetic, chip_gathers(): jnp.stack([jnp.dot(normed, wq[i], preferred_element_type=jnp.float32) for...  10.4 us
    slice x1, local copies, waits for them, and re-layouts, chip_gathers(): wq[i]  8.54 us
    reshape x1, local copies, waits for them, and re-layouts, on_device(): merged = residual.reshape(tok_count // 4, 4 * width_in)  6.69 us
  transfers between devices with their start and end apart: 2, of which 1 were waited for; matrix products, arithmetic and copies ran while one was open for 2% of the time, Pallas kernels for 0%

profile of v1, /device:TPU:0, one launch (start us, length us, event | category | flops | bytes accessed | tf_op | source)
XLA Modules:
  0.0 331.1 jit_solution(8597949088951232956)
XLA Ops:
  0.7 2.0 pad_maximum_fusion.1
  2.7 2.8 reshape.356
  5.5 1.8 broadcast_select_fusion
  7.3 1.9 select_n.217
  9.7 2.5 convert_reduce_fusion
  14.2 2.0 fusion.13
  16.2 1.4 reshape.357
  17.6 1.3 bitcast_select_fusion.1
  20.9 54.0 %shard_map.112 = bf16[2,16,104,1536]{3,2,1,0:T(8,128)(2,1)} custom-call(bf16[104,1536]{1,0:T(8,128)(2,1)} %copy.24.src_ref), custom_call_target="tpu_custom_call" | custom-call | tf_op jit(solution)/shard_map/pallas_call | solution.py:232
  74.9 8.5 %fusion.38 = (bf16[1,16,104,1536]{3,2,1,0:T(8,128)(2,1)}, bf16[1,16,104,1536]{3,2,1,0:T(8,128)(2,1)}) fusion(bf16[2,16,104,1536]{3,2,1,0:T(8,128)(2,1)} %shard_map.112), kind=kLoop, calls=%fused_computation.114 | loop fusion | bytes 20447232 | tf_op jit(solution)/shard_map/slice | solution.py:427
  83.4 11.3 %convolution_bitcast_fusion.1 = f32[1,1024,1536]{2,1,0:T(8,128)} fusion(bf16[1664,1536]{1,0:T(8,128)(2,1)} %bitcast.61, bf16[1024,1664]{1,0:T(8,128)(2,1)} %param.9, f32[1664]{0:T(1024)S(1)} %copy-done.9, f32[1024]{0:T(1024)S(1)} %add_rsqrt_fusion, f32[1024]{0:T(1024)S(1)} %broadcast_multiply_fusion), kind=kOutput, calls=%fused_computation.12 | convolution fusion | flops 5243011072 | bytes 14825984 | tf_op jit(solution)/shard_map/dot_general | solution.py:427
  94.8 8.1 %convolution_bitcast_fusion = f32[1,1024,1536]{2,1,0:T(8,128)} fusion(bf16[1664,1536]{1,0:T(8,128)(2,1)S(1)} %bitcast.60, bf16[1024,1664]{1,0:T(8,128)(2,1)S(1)} %copy-done.4, f32[1664]{0:T(1024)S(1)} %copy-done.9, f32[1024]{0:T(1024)S(1)} %add_rsqrt_fusion, f32[1024]{0:T(1024)S(1)} %broadcast_multiply_fusion), kind=kOutput, calls=%fused_computation.11 | convolution fusion | flops 5243011072 | bytes 14825984 | tf_op jit(solution)/shard_map/dot_general | solution.py:427
  102.9 10.4 %pad_maximum_fusion.mixed_ref = f32[2,1024,1536]{2,1,0:T(8,128)} fusion(f32[1,1024,1536]{2,1,0:T(8,128)} %convolution_bitcast_fusion, f32[1,1024,1536]{2,1,0:T(8,128)} %convolution_bitcast_fusion.1), kind=kLoop, calls=%fused_computation.1 | loop fusion | flops 3145728 | bytes 25165824 | tf_op jit(solution)/shard_map/stack | solution.py:426
  113.4 147.7 %shard_map.113 = (bf16[1024,1024]{1,0:T(8,128)(2,1)S(1)}, f32[1024,128]{1,0:T(8,128)S(1)}, bf16[2,16,104,512]{3,2,1,0:T(8,128)(2,1)}, bf16[16,2,208,2048]{3,2,1,0:T(8,128)(2,1)}) custom-call(f32[2,1024,1536]{2,1,0:T(8,128)} %pad_maximum_fusion.mixed_ref, f32[1024,128]{1,0:T(8,128)S(1)} %get-tuple-element.27.cos_ref, ...), custom_call_target="tpu_custom_call" | custom-call | tf_op jit(solution)/shard_map/pallas_call | solution.py:349
  261.0 2.2 fusion.39
  263.2 2.1 fusion.7
  265.4 3.9 %fusion.5 = bf16[1024,1664]{1,0:T(8,128)(2,1)} fusion(bf16[1024,1664]{1,0:T(8,128)(2,1)S(1)} %copy-done.5, f32[1024,1664]{1,0:T(8,128)S(1)} %fusion.7, bf16[1664,512]{1,0:T(8,128)(2,1)S(1)} %bitcast.59, bf16[1024,1024]{1,0:T(8,128)(2,1)S(1)} %get-tuple-element.7), kind=kOutput, calls=%fused_computation.10 | convolution fusion | flops 1751646208 | bytes 16384000 | tf_op jit(solution)/shard_map/dot_general | solution.py:437
  269.3 6.7 %reshape.361 = bf16[256,6656]{1,0:T(8,128)(2,1)} reshape(bf16[1024,1664]{1,0:T(8,128)(2,1)} %fusion.5) | data formatting | bytes 6815744 | tf_op jit(solution)/shard_map/reshape | solution.py:460
  276.0 14.2 %multiply_reduce_fusion = (f32[256]{0:T(256)S(1)}, bf16[256,2048]{1,0:T(8,128)(2,1)}) fusion(bf16[256,6656]{1,0:T(8,128)(2,1)} %reshape.361, bf16[6656,2048]{1,0:T(8,128)(2,1)} %bitcast.66), kind=kOutput, calls=%fused_computation.13 | convolution fusion | flops 6980894720 | bytes 31720448 | tf_op jit(solution)/shard_map/dot_general | solution.py:461
  291.1 1.3 concatenate.11
  292.4 2.3 gather_fusion
  294.8 2.5 reshape.366
  297.3 6.4 %all-to-all-start = ((bf16[32,4,2,2048]{3,2,1,0:T(2,128)(2,1)}), bf16[32,4,2,2048]{3,2,1,0:T(2,128)(2,1)S(1)}, u32[]{:S(2)}, u32[]{:S(2)}) async-start(bf16[32,4,2,2048]{3,2,1,0:T(2,128)(2,1)} %reshape.366), calls=%async_computation | async-start | bytes 2097152 | tf_op jit(solution)/shard_map/all_to_all | solution.py:469
  304.5 25.4 %all-to-all-done = bf16[32,4,2,2048]{3,2,1,0:T(2,128)(2,1)S(1)} async-done(((bf16[32,4,2,2048]{3,2,1,0:T(2,128)(2,1)}), bf16[32,4,2,2048]{3,2,1,0:T(2,128)(2,1)S(1)}, u32[]{:S(2)}, u32[]{:S(2)}) %all-to-all-start) | async-done | bytes 1048608 | tf_op jit(solution)/shard_map/all_to_all | solution.py:469
  (52 shorter events, 7.4 us)
Async XLA Ops:
  0.6 11.6 %copy-start.3 = (bf16[1024,1664]{1,0:T(8,128)(2,1)S(1)}, bf16[1024,1664]{1,0:T(8,128)(2,1)}, u32[]{:S(2)}) copy-start(bf16[1024,1664]{1,0:T(8,128)(2,1)} %param.9) | copy-start | bytes 10223620
  0.6 12.6 %copy-start.7 = (s32[4,2]{0,1:T(2,128)S(1)}, s32[4,2]{0,1:T(2,128)}, u32[]{:S(2)}) copy-start(s32[4,2]{0,1:T(2,128)} %param.16) | copy-start | bytes 100
  0.7 12.8 %copy-start.1 = (s32[1024]{0:T(1024)S(1)}, s32[1024]{0:T(1024)}, u32[]{:S(2)}) copy-start(s32[1024]{0:T(1024)} %param.14) | copy-start | bytes 12292
  0.7 13.3 %copy-start.8 = (s32[4]{0:T(128)S(1)}, s32[4]{0:T(128)}, u32[]{:S(2)}) copy-start(s32[4]{0:T(128)} %param.17) | copy-start | bytes 52
  9.2 7.0 %collective-permute-start = (bf16[52,1664]{1,0:T(8,128)(2,1)}, bf16[52,1664]{1,0:T(8,128)(2,1)}, u32[]{:S(2)}, u32[]{:S(2)}) collective-permute-start(bf16[52,1664]{1,0:T(8,128)(2,1)} %select_n.217), channel_id=1, source_target_pairs={{0,1},{1,0},{2,3},{3,2},{4,5},{5,4},{6,7},{7,6},{8,9},{9,8},{10,11... | collective-permute-start | bytes 519176 | tf_op jit(solution)/shard_map/ppermute | solution.py:376
  74.9 8.6 %copy-start.9 = (f32[1664]{0:T(1024)S(1)}, f32[1664]{0:T(1024)}, u32[]{:S(2)}) copy-start(f32[1664]{0:T(1024)} %param.10) | copy-start | bytes 19972
  83.4 11.3 %copy-start.4 = (bf16[1024,1664]{1,0:T(8,128)(2,1)S(1)}, bf16[1024,1664]{1,0:T(8,128)(2,1)}, u32[]{:S(2)}) copy-start(bf16[1024,1664]{1,0:T(8,128)(2,1)} %param.9) | copy-start | bytes 10223620
  83.4 11.4 %copy-start.6 = (bf16[1,16,104,1536]{3,2,1,0:T(8,128)(2,1)S(1)}, bf16[1,16,104,1536]{3,2,1,0:T(8,128)(2,1)}, u32[]{:S(2)}) copy-start(bf16[1,16,104,1536]{3,2,1,0:T(8,128)(2,1)} %get-tuple-element.18) | copy-start | bytes 15335428
  102.9 10.5 %copy-start = (bf16[208,2048]{1,0:T(8,128)(2,1)S(1)}, bf16[208,2048]{1,0:T(8,128)(2,1)}, u32[]{:S(2)}) copy-start(bf16[208,2048]{1,0:T(8,128)(2,1)} %wp_ref.1) | copy-start | bytes 2555908
  102.9 10.4 %copy-start.2 = (s32[1024]{0:T(1024)S(1)}, s32[1024]{0:T(1024)}, u32[]{:S(2)}) copy-start(s32[1024]{0:T(1024)} %param.15) | copy-start | bytes 12292
  263.2 2.1 copy-start.5
  297.3 32.6 %all-to-all-start = ((bf16[32,4,2,2048]{3,2,1,0:T(2,128)(2,1)}), bf16[32,4,2,2048]{3,2,1,0:T(2,128)(2,1)S(1)}, u32[]{:S(2)}, u32[]{:S(2)}) async-start(bf16[32,4,2,2048]{3,2,1,0:T(2,128)(2,1)} %reshape.366), calls=%async_computation | async-start | bytes 2097152 | tf_op jit(solution)/shard_map/all_to_all | solution.py:469

commit v2 on v1

--- a/solution.py
+++ b/solution.py
@@ -211,90 +211,83 @@
             gathers[step - 4].finish()
 
 
-def qkv_kernel(chunks, src_ref, out_ref, *sems):
-    place = Place()
-    place.greet()
-    wide = src_ref.shape[1] // chunks
-    gathers = []
-    for q in range(chunks):
-        cols = slice(q * wide, (q + 1) * wide)
-
-        def dst_of(chip, cols=cols):
-            return out_ref.at[place.core, chip, :, cols]
-
-        gathers.append(Gather(place, src_ref.at[:, cols], dst_of, sems, q))
-    run_gathers(gathers, lambda step: None)
-
-
-def gather_qkv(block):
-    rows, cols = block.shape
-    chunks = 4
-    return pl.pallas_call(
-        functools.partial(qkv_kernel, chunks),
-        out_shape=jax.ShapeDtypeStruct((2, 16, rows, cols), block.dtype),
-        in_specs=[pl.BlockSpec(memory_space=pl.ANY)],
-        out_specs=pl.BlockSpec(memory_space=pl.ANY),
-        scratch_shapes=gather_sems(chunks),
-        compiler_params=pltpu.CompilerParams(collective_id=0, has_side_effects=True),
-    )(block)
-
-
 def attend_kernel(
-    chunks,
+    q_chunks,
+    p_chunks,
     scale,
-    mixed_ref,
+    patches_ref,
+    gain_ref,
     cos_ref,
     sin_a_ref,
     sin_b_ref,
     seg_col_ref,
     seg_row_ref,
     mask_row_ref,
+    wq_ref,
     wo_ref,
     wp_ref,
     att_ref,
     top_ref,
+    wq_all,
     wo_all,
     wp_all,
+    wq_buf,
     q_buf,
     k_buf,
     v_buf,
+    load_sem,
     *sems,
 ):
     place = Place()
     place.greet()
-    wide = wp_ref.shape[1] // chunks
-    gathers = [
-        Gather(place, wo_ref, lambda chip: wo_all.at[place.core, chip], sems, 0)
-    ]
-    for q in range(chunks):
+    depth, wq_cols = wq_ref.shape
+    gathers = []
+    wide = wq_cols // q_chunks
+    for q in range(q_chunks):
+        cols = slice(q * wide, (q + 1) * wide)
+
+        def dst_of(chip, cols=cols):
+            rows = pl.ds(pl.multiple_of(chip * depth, 8), depth)
+            return wq_all.at[place.core, rows, cols]
+
+        gathers.append(Gather(place, wq_ref.at[:, cols], dst_of, sems, len(gathers)))
+    gathers.append(
+        Gather(place, wo_ref, lambda chip: wo_all.at[place.core, chip], sems, len(gathers))
+    )
+    wide = wp_ref.shape[1] // p_chunks
+    for q in range(p_chunks):
         cols = slice(q * wide, (q + 1) * wide)
 
         def dst_of(chip, cols=cols):
             return wp_all.at[chip, place.core, :, cols]
 
-        gathers.append(Gather(place, wp_ref.at[:, cols], dst_of, sems, q + 1))
-    tokens = seg_col_ref.shape[0]
+        gathers.append(Gather(place, wp_ref.at[:, cols], dst_of, sems, len(gathers)))
+    tokens, width = patches_ref.shape
     block = 256
     half = HEADS // 2
-
-    def turn(i, carry):
+    quarter = 26
+
+    def project(i, carry):
         rows = pl.ds(pl.multiple_of(i * block, block), block)
+        tokens_f = patches_ref[rows, :].astype(jnp.float32)
+        centered = tokens_f - jnp.mean(tokens_f, axis=1, keepdims=True)
+        var = jnp.mean(centered * centered, axis=1, keepdims=True)
+        normed = (centered * lax.rsqrt(var + 1e-06) * gain_ref[...]).astype(jnp.bfloat16)
         cosine, sin_a, sin_b = cos_ref[rows, :], sin_a_ref[rows, :], sin_b_ref[rows, :]
-        quarter = 26
-        for h in range(HEADS):
-            at = (h % half) * LANES
-            out = slice(h * LANES, (h + 1) * LANES)
-            for kind, buf in ((0, q_buf), (1, k_buf)):
-                lanes = slice(kind * half * LANES + at, kind * half * LANES + at + LANES)
-                val = mixed_ref[h // half, rows, lanes]
-                turned = (
-                    val * cosine
-                    + pltpu.roll(val, LANES - quarter, 1) * sin_a
-                    + pltpu.roll(val, quarter, 1) * sin_b
-                )
-                buf[rows, out] = turned.astype(jnp.bfloat16)
-            lanes = slice(2 * half * LANES + at, 2 * half * LANES + at + LANES)
-            v_buf[rows, out] = mixed_ref[h // half, rows, lanes].astype(jnp.bfloat16)
+        for part in range(2):
+            mixed = jnp.dot(normed, wq_buf[part], preferred_element_type=jnp.float32)
+            for kind, buf in ((0, q_buf), (1, k_buf), (2, v_buf)):
+                for h in range(half):
+                    at = (kind * half + h) * LANES
+                    val = mixed[:, at : at + LANES]
+                    if kind < 2:
+                        val = (
+                            val * cosine
+                            + pltpu.roll(val, LANES - quarter, 1) * sin_a
+                            + pltpu.roll(val, quarter, 1) * sin_b
+                        )
+                    out = (part * half + h) * LANES
+                    buf[rows, out : out + LANES] = val.astype(jnp.bfloat16)
         return carry
 
     def one_block(i, carry):
@@ -328,39 +321,60 @@
         return carry
 
     blocks = tokens // block
+    loaded = q_chunks + 4
 
     def work(step):
-        if step == 0:
-            lax.fori_loop(0, blocks, turn, 0)
-        elif step == 1:
+        if step == loaded:
+            load = pltpu.make_async_copy(wq_all, wq_buf, load_sem)
+            load.start()
+            load.wait()
+            lax.fori_loop(0, blocks // 2, project, 0)
+        elif step == loaded + 1:
+            lax.fori_loop(blocks // 2, blocks, project, 0)
+        elif step == loaded + 2:
             lax.fori_loop(0, blocks // 2, one_block, 0)
-        elif step == 2:
+        elif step == loaded + 3:
             lax.fori_loop(blocks // 2, blocks, one_block, 0)
 
     run_gathers(gathers, work)
 
 
-def attend_and_gather(mixed, tables, seg, mask, wo_block, w_proj, head_dim):
-    tokens = seg.shape[0]
-    chunks = 4
+def attend_and_gather(patches, gain, tables, seg, mask, wq_block, wo_block, w_proj, head_dim):
+    tokens, width = patches.shape
+    q_chunks, p_chunks = 4, 8
     wide = HEADS * LANES
     vmem = pl.BlockSpec(memory_space=pltpu.VMEM)
     hbm = pl.BlockSpec(memory_space=pl.ANY)
+    wq_shape = (2, width, wq_block.shape[1])
     return pl.pallas_call(
-        functools.partial(attend_kernel, chunks, head_dim ** (-0.5)),
+        functools.partial(attend_kernel, q_chunks, p_chunks, head_dim ** (-0.5)),
         out_shape=(
             jax.ShapeDtypeStruct((tokens, wide), jnp.bfloat16),
             jax.ShapeDtypeStruct((tokens, LANES), jnp.float32),
+            jax.ShapeDtypeStruct(wq_shape, jnp.bfloat16),
             jax.ShapeDtypeStruct((2, 16) + wo_block.shape, jnp.bfloat16),
             jax.ShapeDtypeStruct((16, 2) + w_proj.shape, jnp.bfloat16),
         ),
-        in_specs=[vmem] * 7 + [hbm] * 2,
-        out_specs=(vmem, vmem, hbm, hbm),
-        scratch_shapes=[pltpu.VMEM((tokens, wide), jnp.bfloat16)] * 3 + gather_sems(chunks + 1),
+        in_specs=[vmem] * 8 + [hbm] * 3,
+        out_specs=(vmem, vmem, hbm, hbm, hbm),
+        scratch_shapes=[pltpu.VMEM(wq_shape, jnp.bfloat16)]
+        + [pltpu.VMEM((tokens, wide), jnp.bfloat16)] * 3
+        + [pltpu.SemaphoreType.DMA]
+        + gather_sems(q_chunks + 1 + p_chunks),
         compiler_params=pltpu.CompilerParams(
-            collective_id=1, has_side_effects=True, vmem_limit_bytes=48 * 1024 * 1024
+            collective_id=1, has_side_effects=True, vmem_limit_bytes=56 * 1024 * 1024
         ),
-    )(mixed, *tables, seg[:, None], seg[None, :], mask[None, :], wo_block, w_proj)
+    )(
+        patches,
+        gain[None, :],
+        *tables,
+        seg[:, None],
+        seg[None, :],
+        mask[None, :],
+        wq_block,
+        wo_block,
+        w_proj,
+    )
 
 
 def pair_blocks(w_qkv, w_out, head_dim):
@@ -381,8 +395,13 @@
     return both[:, :3].reshape(2 * rows, 3 * half * LANES), both[:, 3]
 
 
-def plain_gathers(normed, tables, seg_ids, patch_mask, w_qkv, w_out, w_proj):
-    tok_count = normed.shape[0]
+def plain_gathers(patches, ln_gain, tables, seg_ids, patch_mask, w_qkv, w_out, w_proj):
+    tok_count = patches.shape[0]
+    tokens_f = patches.astype(jnp.float32)
+    mean_row = jnp.mean(tokens_f, axis=-1, keepdims=True)
+    centered = tokens_f - mean_row
+    var_row = jnp.mean(centered * centered, axis=-1, keepdims=True)
+    normed = (centered * lax.rsqrt(var_row + 1e-06) * ln_gain).astype(jnp.bfloat16)
     hidden_w = w_out.shape[0]
     head_dim = hidden_w // HEADS
     quarter = head_dim // 4
@@ -419,15 +438,11 @@
     return out_term, jnp.max(masked, axis=(0, 2)), lax.all_gather(w_proj, "dp", axis=0, tiled=True)
 
 
-def chip_gathers(normed, tables, seg_ids, patch_mask, w_qkv, w_out, w_proj):
+def chip_gathers(patches, ln_gain, tables, seg_ids, patch_mask, w_qkv, w_out, w_proj):
     head_dim = w_out.shape[0] // HEADS
-    qkv_block, wo_block = pair_blocks(w_qkv, w_out, head_dim)
-    wq = gather_qkv(qkv_block).reshape(2, -1, qkv_block.shape[1])
-    mixed = jnp.stack(
-        [jnp.dot(normed, wq[i], preferred_element_type=jnp.float32) for i in range(2)]
-    )
-    att, top, wo, wp = attend_and_gather(
-        mixed, tables, seg_ids, patch_mask, wo_block, w_proj, head_dim
+    wq_block, wo_block = pair_blocks(w_qkv, w_out, head_dim)
+    att, top, _, wo, wp = attend_and_gather(
+        patches, ln_gain, tables, seg_ids, patch_mask, wq_block, wo_block, w_proj, head_dim
     )
     wo = wo.reshape(2, -1, wo_block.shape[1])
     span = wo.shape[2]
@@ -445,15 +460,13 @@
     proj_w = w_proj.shape[1]
     devices = lax.axis_size("dp")
     tokens_f = patches.astype(jnp.float32)
-    mean_row = jnp.mean(tokens_f, axis=-1, keepdims=True)
-    centered = tokens_f - mean_row
-    var_row = jnp.mean(centered * centered, axis=-1, keepdims=True)
-    normed = (centered * lax.rsqrt(var_row + 1e-06) * ln_gain).astype(jnp.bfloat16)
     row_pos, col_pos, areas, starts = token_places(seg_ids, grid_hw)
     tables = rope_tables(row_pos, col_pos, head_dim)
     image_ids = jnp.arange(image_count, dtype=jnp.int32)
     path = chip_gathers if devices == 32 else plain_gathers
-    out_term, row_top, wp = path(normed, tables, seg_ids, patch_mask, w_qkv, w_out, w_proj)
+    out_term, row_top, wp = path(
+        patches, ln_gain, tables, seg_ids, patch_mask, w_qkv, w_out, w_proj
+    )
     member_q = seg_ids[:, None] == image_ids[None, :]
     top_logit = jnp.max(jnp.where(member_q, row_top[:, None], -1e30), axis=0)
     residual = (tokens_f + out_term).astype(jnp.bfloat16)

time: 332 us -> 265 us (0.80)
  matrix products: 39.7 us -> 17.8 us
  other arithmetic: 23.3 us -> 8.27 us
  Pallas kernels: 202 us -> 187 us
  local copies, waits for them, and re-layouts: 33.3 us -> 18.7 us
    dot_general x2 -> x0, matrix products: 19.5 us -> none  [chip_gathers(): jnp.dot(normed, wq[i], preferred_element_type=jnp.float32)]
    pallas_call x2 -> x1, Pallas kernels: 202 us -> 187 us  [attend_and_gather(): pl.pallas_call(functools.partial(attend_kernel, q_chunks, p_chunks, head_...]
    another operation x2 -> x1, other arithmetic: 10.6 us -> 0.18 us  [the longest x1 10.4 us: chip_gathers(): jnp.stack([jnp.dot(normed, wq[i], preferred_element_type=jnp.float32) for...]
    slice x1 -> x0, local copies, waits for them, and re-layouts: 8.54 us -> none  [chip_gathers(): wq[i]]
    reduce_sum x2 -> x0, other arithmetic: 3.51 us -> none  [the longest x1 2.48 us: on_device(): mean_row = jnp.mean(tokens_f, axis=-1, keepdims=True)]
  transfers between devices with their start and end apart: 2 -> 2, of which waited for: 1 -> 1; matrix products, arithmetic and copies ran while one was open for 2% -> 4% of each run, Pallas kernels for 0% -> 0%
where the time goes in v2:
time: 265 us; the launch traced here: 264 us
  Pallas kernels  187 us (71%)
  waiting for transfers between devices  25.4 us (10%)
  local copies, waits for them, and re-layouts  18.7 us (7%)
  matrix products  17.8 us (7%)
  other arithmetic  8.27 us (3%)
  starting transfers between devices  6.74 us (3%)
    pallas_call x1, Pallas kernels, attend_and_gather(): pl.pallas_call(functools.partial(attend_kernel, q_chunks, p_chunks, head_...  187 us
    all_to_all x1, waiting for transfers between devices, on_device(): lax.all_to_all(sent, 'dp', split_axis=0, concat_axis=0, tiled=True)  25.4 us
    dot_general x1, matrix products, on_device(): projected = jnp.dot(merged, wp, preferred_element_type=jnp.float32)  13.5 us
    all_to_all x1, starting transfers between devices, on_device(): lax.all_to_all(sent, 'dp', split_axis=0, concat_axis=0, tiled=True)  6.22 us
  transfers between devices with their start and end apart: 2, of which 1 were waited for; matrix products, arithmetic and copies ran while one was open for 4% of the time, Pallas kernels for 0%

profile of v2, /device:TPU:0, one launch (start us, length us, event | category | flops | bytes accessed | tf_op | source)
XLA Modules:
  0.0 264.4 jit_solution(9023234621347544358)
XLA Ops:
  0.7 1.1 pad_maximum_fusion
  1.8 1.1 reshape.339
  3.2 0.5 collective-permute-start
  3.8 0.8 slice_multiply_fusion
  4.8 0.8 and_select_fusion
  5.5 0.8 reshape.346
  6.4 1.7 copy.24.seg_col_ref
  8.1 1.3 broadcast_in_dim.125.gain_ref
  9.7 3.2 %fusion.7 = (f32[1024,128]{1,0:T(8,128)}, f32[1024,128]{1,0:T(8,128)}, f32[1024,128]{1,0:T(8,128)}) fusion(f32[128]{0:T(128)S(1)} %fusion.28, f32[1024]{0:T(1024)S(1)} %get-tuple-element.27, f32[1024]{0:T(1024)S(1)} %get-tuple-element.26, pred[128]{0:T(512)(128)(4,1)S(1)} %get-tuple-element.30, pred[128]{0:T(512)(128)(4,1)S(1)} %broadcast_compare_fusion, ...), kind=kLoop, calls=%fused_computation.14 | loop fusion | flops 655360 | bytes 1581952 | tf_op jit(solution)/shard_map/jit(_where)/select_n | solution.py:48
  14.6 0.9 copy.25.wq_ref
  15.5 0.7 copy.31
  16.1 186.6 %shard_map.112 = (bf16[1024,1024]{1,0:T(8,128)(2,1)}, f32[1024,128]{1,0:T(8,128)}, bf16[2,1664,1536]{2,1,0:T(8,128)(2,1)}, bf16[2,16,104,512]{3,2,1,0:T(8,128)(2,1)}, bf16[16,2,208,2048]{3,2,1,0:T(8,128)(2,1)}) custom-call(bf16[1024,1664]{1,0:T(8,128)(2,1)} %patches_ref.1, f32[1,1664]{1,0:T(1,128)} %broadcast_in_dim.125.gain_ref, ...), custom_call_target="tpu_custom_call" | custom-call | tf_op jit(solution)/shard_map/pallas_call | solution.py:349
  202.7 2.3 fusion.30
  205.3 2.1 fusion.1
  207.5 2.2 add_convert_fusion
  209.7 3.6 %reshape.343 = bf16[256,6656]{1,0:T(8,128)(2,1)} reshape(bf16[1024,1664]{1,0:T(8,128)(2,1)S(1)} %add_convert_fusion) | data formatting | bytes 6815744 | tf_op jit(solution)/shard_map/reshape | solution.py:473
  213.3 13.5 %multiply_reduce_fusion = (f32[256]{0:T(256)S(1)}, bf16[256,2048]{1,0:T(8,128)(2,1)S(1)}) fusion(bf16[256,6656]{1,0:T(8,128)(2,1)} %reshape.343, bf16[6656,2048]{1,0:T(8,128)(2,1)} %bitcast.56), kind=kOutput, calls=%fused_computation.2 | convolution fusion | flops 6980894720 | bytes 31720448 | tf_op jit(solution)/shard_map/dot_general | solution.py:474
  226.9 0.5 fusion.29
  227.9 1.4 gather_fusion
  229.3 1.5 reshape.348
  230.8 6.2 %all-to-all-start = ((bf16[32,4,2,2048]{3,2,1,0:T(2,128)(2,1)}), bf16[32,4,2,2048]{3,2,1,0:T(2,128)(2,1)S(1)}, u32[]{:S(2)}, u32[]{:S(2)}) async-start(bf16[32,4,2,2048]{3,2,1,0:T(2,128)(2,1)} %reshape.348), calls=%async_computation | async-start | bytes 2097152 | tf_op jit(solution)/shard_map/all_to_all | solution.py:482
  237.2 0.6 select_reduce_fusion
  237.9 25.4 %all-to-all-done = bf16[32,4,2,2048]{3,2,1,0:T(2,128)(2,1)S(1)} async-done(((bf16[32,4,2,2048]{3,2,1,0:T(2,128)(2,1)}), bf16[32,4,2,2048]{3,2,1,0:T(2,128)(2,1)S(1)}, u32[]{:S(2)}, u32[]{:S(2)}) %all-to-all-start) | async-done | bytes 1048608 | tf_op jit(solution)/shard_map/all_to_all | solution.py:482
  263.2 1.2 reshape.345
  (38 shorter events, 3.6 us)
Async XLA Ops:
  0.6 8.8 %copy-start.3 = (s32[1024]{0:T(1024)S(1)}, s32[1024]{0:T(1024)}, u32[]{:S(2)}) copy-start(s32[1024]{0:T(1024)} %param.14) | copy-start | bytes 12292
  0.6 12.2 %copy-start.6 = (s32[4]{0:T(128)S(1)}, s32[4]{0:T(128)}, u32[]{:S(2)}) copy-start(s32[4]{0:T(128)} %param.17) | copy-start | bytes 52
  3.2 9.6 %collective-permute-start = (bf16[52,1664]{1,0:T(8,128)(2,1)S(1)}, bf16[52,1664]{1,0:T(8,128)(2,1)S(1)}, u32[]{:S(2)}, u32[]{:S(2)}) collective-permute-start(bf16[52,1664]{1,0:T(8,128)(2,1)S(1)} %select_n.232), channel_id=1, source_target_pairs={{0,1},{1,0},{2,3},{3,2},{4,5},{5,4},{6,7},{7,6},{8,9},{9,8},{10,11... | collective-permute-start | bytes 519176 | tf_op jit(solution)/shard_map/ppermute | solution.py:390
  202.7 2.6 copy-start.1
  205.3 2.1 copy-start
  213.3 13.6 %copy-start.5 = (s32[4,2]{0,1:T(2,128)S(1)}, s32[4,2]{0,1:T(2,128)}, u32[]{:S(2)}) copy-start(s32[4,2]{0,1:T(2,128)} %param.16) | copy-start | bytes 100
  229.2 7.8 %copy-start.2 = (f32[1024,128]{1,0:T(8,128)S(1)}, f32[1024,128]{1,0:T(8,128)}, u32[]{:S(2)}) copy-start(f32[1024,128]{1,0:T(8,128)} %get-tuple-element.10) | copy-start | bytes 1572868
  229.3 8.0 %copy-start.4 = (s32[1024]{0:T(1024)S(1)}, s32[1024]{0:T(1024)}, u32[]{:S(2)}) copy-start(s32[1024]{0:T(1024)} %param.14) | copy-start | bytes 12292
  230.8 32.5 %all-to-all-start = ((bf16[32,4,2,2048]{3,2,1,0:T(2,128)(2,1)}), bf16[32,4,2,2048]{3,2,1,0:T(2,128)(2,1)S(1)}, u32[]{:S(2)}, u32[]{:S(2)}) async-start(bf16[32,4,2,2048]{3,2,1,0:T(2,128)(2,1)} %reshape.348), calls=%async_computation | async-start | bytes 2097152 | tf_op jit(solution)/shard_map/all_to_all | solution.py:482
